TPU v7x, 512 devices: a whole 4x4x16 slice. The times are simulated.
512 devices in a mesh: section: 16 (over x, y_lo, core), expert: 32 (over y_hi, z).
Axes of the slice: x: 4, y: 4 (y_hi: 2, y_lo: 2; y = y_hi * 2 + y_lo), z: 16, core: 2. Of those that a mesh axis runs over, the one named last changes fastest.
Arguments:
- tokens: bfloat16 [16, 2048, 3584], P('section', 'expert'), may hold values from -25 to 25
- norm_gain: bfloat16 [16, 3584], P('section'), may hold values from 0.25 to 1.75
- w_gate: bfloat16 [16, 3584, 4096], P('section', None, 'expert'), may hold values from -0.09375 to 0.09375
- w_up: bfloat16 [16, 3584, 4096], P('section', None, 'expert'), may hold values from -0.09375 to 0.09375
- w_down: bfloat16 [16, 4096, 3584], P('section', 'expert'), may hold values from -0.1875 to 0.1875
- expert_ids: int32 [16, 2048, 2], P('section', 'expert'), may hold values from 0 to 3, as said below
- slot_ids: int32 [16, 2048, 2], P('section', 'expert'), may hold values from 0 to 55, as said below
- route_weight: float32 [16, 2048, 2], P('section', 'expert'), may hold values from 0.2 to 1.2
Outputs:
- next_input: bfloat16 [16, 2048, 3584], P('section', 'expert')
Inputs may be any that keep to these rules, and one draw needn't show every extreme that they name: `expert_ids`: each token names 2 different experts. In the rows of one block of 64 tokens (one index of expert in one section) the slots of one expert are 0, 1, 2 and so on in token order, one per token that names it, so the pairs of expert and slot are distinct; one expert, the same in every block, is named by exactly 56 tokens of every block. `slot_ids`: see expert_ids: slots count up from 0 for each expert within the rows of one block.
All inputs are finite; a program needn't handle non-finite values.
Results may differ from a plain program's by a relative error of at most 0.0049.
Values may be sent and summed in bfloat16 or wider, within the bound.
No kernel may reach another device: no remote copies, remote signals or barrier semaphores. Data moves between devices by JAX's collectives and lax.ppermute only.
A program may use at most 128 MiB of HBM per device.

v0:
```python
import jax
import jax.numpy as jnp
from jax import lax
from jax.sharding import PartitionSpec as P

EXPERTS = 4
CAP = 56


def from_behind(value, axis, steps):
    count = lax.axis_size(axis)
    pairs = [(source, (source + steps) % count) for source in range(count)]
    return lax.ppermute(value, axis, pairs)


def local(tokens, norm_gain, w_gate, w_up, w_down, expert_ids, slot_ids, route_weight):
    members = lax.axis_size("expert")
    groups = members // EXPERTS
    width = tokens.shape[2]
    values = tokens[0].astype(jnp.float32)
    mean_sq = jnp.mean(values * values, axis=-1, keepdims=True)
    normed = (values * lax.rsqrt(mean_sq + 1e-06) * norm_gain[0].astype(jnp.float32)).astype(
        jnp.bfloat16
    )
    codes = expert_ids[0] * CAP + slot_ids[0]
    columns = jnp.arange(EXPERTS * CAP, dtype=jnp.int32)
    expert_match_mask = codes[:, :, None] == columns
    gate_local = w_gate[0]
    up_local = w_up[0]
    down_local = w_down[0]
    hid_cols = down_local.shape[0]
    expert_selector_index = jnp.sum(expert_match_mask.astype(jnp.bfloat16), axis=1)
    packed = jnp.einsum(
        "tq,td->qd", expert_selector_index, normed, preferred_element_type=jnp.float32
    ).astype(jnp.bfloat16)
    packed = packed.reshape(EXPERTS, 1, CAP, width)
    outgoing = jnp.broadcast_to(packed, (EXPERTS, groups, CAP, width)).reshape(members, CAP, width)
    received = lax.all_to_all(outgoing, "expert", split_axis=0, concat_axis=0, tiled=True)
    flat_rows = received.reshape(-1, width)
    gate_part = jnp.dot(flat_rows, gate_local, preferred_element_type=jnp.float32)
    up_part = jnp.dot(flat_rows, up_local, preferred_element_type=jnp.float32)
    hidden = (jax.nn.silu(gate_part) * up_part).astype(jnp.bfloat16)
    hidden = hidden.reshape(received.shape[:-1] + (hid_cols,)).reshape(-1, hid_cols)
    partial_value = jnp.dot(hidden, down_local, preferred_element_type=jnp.float32).astype(
        jnp.bfloat16
    )
    finished = partial_value.reshape(received.shape)
    returned = lax.all_to_all(finished, "expert", split_axis=0, concat_axis=0, tiled=True)
    summed = jnp.sum(
        returned.astype(jnp.float32).reshape(EXPERTS, groups, CAP, width), axis=1
    ).reshape(EXPERTS * CAP, width)
    weights = route_weight[0][:, :, None]
    gate_mixing_weight = jnp.sum(
        jnp.where(expert_match_mask, weights, jnp.zeros_like(weights)), axis=1
    )
    residual_branch = jnp.dot(
        gate_mixing_weight,
        summed,
        precision=lax.Precision.HIGHEST,
        preferred_element_type=jnp.float32,
    )
    mixed = (values + residual_branch).astype(jnp.bfloat16)[None]
    return from_behind(mixed, "section", 1)


def solution(mesh):
    placed = (
        P("section", "expert", None),
        P("section", None),
        P("section", None, "expert"),
        P("section", None, "expert"),
        P("section", "expert", None),
        P("section", "expert", None),
        P("section", "expert", None),
        P("section", "expert", None),
    )
    return jax.shard_map(
        local, mesh=mesh, in_specs=placed, out_specs=P("section", "expert", None), check_vma=False
    )
```

profile of v0, /device:TPU:164, one launch (start us, length us, event | category | flops | bytes accessed | tf_op | source)
XLA Modules:
  0.0 1204.0 jit_solution(14762481166048984978)
XLA Ops:
  0.0 0.0 copy-start
  0.0 0.8 add_bitcast_fusion
  0.8 0.1 fusion.22
  0.9 0.8 convert_reduce_fusion.1
  1.6 1.2 fusion.3
  2.9 1.7 convolution_convert_fusion.1
  4.5 5.5 broadcast_in_dim.37
  10.1 0.0 copy-start.5
  10.1 574.0 %all_to_all.10 = bf16[32,56,3584]{2,1,0:T(8,128)(2,1)S(1)} all-to-all(bf16[32,56,3584]{2,1,0:T(8,128)(2,1)} %bitcast.39), channel_id=1, replica_groups=mesh['section'=16,'expert'=32] {'expert'}, dimensions={0} | all-to-all | bytes 25690112 | tf_op jit(solution)/shard_map/all_to_all | solution.py:38
  584.1 0.0 copy-start.1
  584.1 0.0 copy-start.3
  584.1 4.6 copy-done.1
  588.7 0.0 copy-done.5
  588.7 3.5 fusion.9
  592.2 0.0 copy-done
  592.2 0.0 copy-done.3
  592.2 18.9 %convolution_convert_fusion = bf16[1792,3584]{1,0:T(8,128)(2,1)} fusion(bf16[1792,3584]{1,0:T(8,128)(2,1)} %bitcast.38, bf16[1,128,3584]{2,1,0:T(8,128)(2,1)S(1)} %copy-done, bf16[1,3584,128]{2,1,0:T(8,128)(2,1)S(1)} %copy-done.3, f32[1792,128]{1,0:T(8,128)S(1)} %fusion.9), kind=kOutput, calls=%fused_computation.1 | convolution fusion | flops 3296133120 | bytes 28442624 | tf_op jit(solution)/shard_map/dot_general | solution.py:44
  611.1 0.0 copy-start.4
  611.1 10.5 all-to-all-start.1
  621.6 0.0 copy-start.2
  621.6 0.0 copy-done.4
  621.6 0.1 select_reduce_fusion
  621.7 558.4 %all-to-all-done.1 = bf16[32,56,3584]{2,1,0:T(8,128)(2,1)} async-done(((bf16[32,56,3584]{2,1,0:T(8,128)(2,1)}), bf16[32,56,3584]{2,1,0:T(8,128)(2,1)}, u32[]{:S(2)}, u32[]{:S(2)}) %all-to-all-start.1) | async-done | bytes 12845088 | tf_op jit(solution)/shard_map/all_to_all | solution.py:48
  1180.1 8.4 convert_reduce_fusion
  1188.5 0.0 copy-done.2
  1188.5 4.0 fusion.1
  1192.5 1.9 collective-permute-start
  1194.4 8.8 collective-permute-done
  1203.2 0.8 copy.12
  (1 shorter events, 0.0 us)
Async XLA Ops:
  0.0 592.2 %copy-start = (bf16[1,128,3584]{2,1,0:T(8,128)(2,1)S(1)}, bf16[1,128,3584]{2,1,0:T(8,128)(2,1)}, u32[]{:S(2)}) copy-start(bf16[1,128,3584]{2,1,0:T(8,128)(2,1)} %param.12) | copy-start | bytes 2752516
  10.1 578.6 %copy-start.5 = (bf16[1,3584,128]{2,1,0:T(8,128)(2,1)S(1)}, bf16[1,3584,128]{2,1,0:T(8,128)(2,1)}, u32[]{:S(2)}) copy-start(bf16[1,3584,128]{2,1,0:T(8,128)(2,1)} %param.10) | copy-start | bytes 2752516
  584.1 4.6 copy-start.1
  584.1 8.1 copy-start.3
  611.1 10.5 copy-start.4
  611.1 569.0 %all-to-all-start.1 = ((bf16[32,56,3584]{2,1,0:T(8,128)(2,1)}), bf16[32,56,3584]{2,1,0:T(8,128)(2,1)}, u32[]{:S(2)}, u32[]{:S(2)}) async-start(bf16[32,56,3584]{2,1,0:T(8,128)(2,1)} %bitcast.36), calls=%async_computation.1 | async-start | bytes 25690112 | tf_op jit(solution)/shard_map/all_to_all | solution.py:48
  621.6 567.0 %copy-start.2 = (bf16[1,64,3584]{2,1,0:T(8,128)(2,1)S(1)}, bf16[1,64,3584]{2,1,0:T(8,128)(2,1)}, u32[]{:S(2)}) copy-start(bf16[1,64,3584]{2,1,0:T(8,128)(2,1)} %param.8) | copy-start | bytes 1376260
  1192.5 10.7 collective-permute-start
where the time goes:
time: 1210 us; the launch traced here: 1200 us
  blocking collectives  574 us (47%)
  waiting for transfers between devices  567 us (47%)
  matrix products  28 us (2%)
  starting transfers between devices  12.4 us (1%)
    all_to_all x1, blocking collectives, local(): lax.all_to_all(outgoing, 'expert', split_axis=0, concat_axis=0, tiled=True)  574 us
    all_to_all x1, waiting for transfers between devices, local(): lax.all_to_all(finished, 'expert', split_axis=0, concat_axis=0, tiled=True)  558 us
  transfers between devices with their start and end apart: 2, of which 2 were waited for; matrix products, arithmetic and copies ran while one was open for 0% of the time, Pallas kernels for 0%

commit v1 on v0

v1 whole, which is shorter than its diff:
```python
import jax
import jax.numpy as jnp
from jax import lax
from jax.sharding import Mesh
from jax.sharding import PartitionSpec as P

EXPERTS = 4


def local(tokens, norm_gain, w_gate, w_up, w_down, expert_ids, slot_ids, route_weight):
    row, col = lax.axis_index("row"), lax.axis_index("col")
    rows, cols = lax.axis_size("row"), lax.axis_size("col")
    count, width = tokens.shape[1:]
    swap = [(0, 1), (1, 0)]

    named = expert_ids[0][None] == jnp.arange(EXPERTS, dtype=jnp.int32)[:, None, None]
    dense = jnp.sum(jnp.where(named, route_weight[0][None], 0.0), axis=2)
    spread = jnp.broadcast_to(dense.reshape(1, -1), (cols, EXPERTS * count))
    spread = lax.all_to_all(spread, "col", split_axis=0, concat_axis=0, tiled=True)
    spread = spread.reshape(cols, EXPERTS, count)

    values = tokens[0].astype(jnp.float32)
    mean_sq = jnp.mean(values * values, axis=-1, keepdims=True)
    normed = values * lax.rsqrt(mean_sq + 1e-06) * norm_gain[0].astype(jnp.float32)
    gathered = lax.all_gather(normed.astype(jnp.bfloat16), "col", axis=0, tiled=True)

    gate_far = lax.ppermute(w_gate[0], "row", swap)
    up_far = lax.ppermute(w_up[0], "row", swap)
    down_far = lax.ppermute(w_down[0], "row", swap)
    first = jnp.concatenate([w_gate[0], gate_far, w_up[0], up_far], axis=1)
    second = jnp.concatenate([w_down[0], down_far], axis=0)
    per_row = EXPERTS // rows
    mine = col // (cols // per_row)

    def weight_of(expert):
        picked = lax.dynamic_index_in_dim(spread, expert, 1, keepdims=False)
        return jnp.broadcast_to(picked.reshape(-1, 1), (cols * count, w_gate.shape[2]))

    weights = jnp.concatenate(
        [weight_of(row * per_row + mine), weight_of((1 - row) * per_row + mine)], axis=1
    )
    both = jnp.dot(gathered, first, preferred_element_type=jnp.float32)
    half = both.shape[1] // 2
    hidden = (jax.nn.silu(both[:, :half]) * both[:, half:] * weights).astype(jnp.bfloat16)
    piece = jnp.dot(hidden, second, preferred_element_type=jnp.float32).astype(jnp.bfloat16)
    summed = lax.psum_scatter(piece, "col", scatter_dimension=0, tiled=True)
    mixed = (values + summed.astype(jnp.float32)).astype(jnp.bfloat16)[None]
    sections = lax.axis_size("section")
    return lax.ppermute(mixed, "section", [(i, (i + 1) % sections) for i in range(sections)])


def solution(mesh):
    sections, members = mesh.devices.shape
    fine = Mesh(mesh.devices.reshape(sections, 2, members // 2), ("section", "row", "col"))
    split = ("row", "col")
    placed = (
        P("section", split, None),
        P("section", None),
        P("section", None, split),
        P("section", None, split),
        P("section", split, None),
        P("section", split, None),
        P("section", split, None),
        P("section", split, None),
    )
    return jax.shard_map(
        local, mesh=fine, in_specs=placed, out_specs=P("section", split, None), check_vma=False
    )
```

time: 1210 us -> 240 us (0.20)
  the two profiles are of different devices: /device:TPU:164 before, /device:TPU:16 now
where the time goes in v1:
time: 240 us
  waiting for transfers between devices  177 us (74%)
  starting transfers between devices  26.8 us (11%)
  matrix products  13.8 us (6%)
  between operations  13.5 us (6%)
  other arithmetic  5.81 us (2%)
    reduce_scatter x1, waiting for transfers between devices, local(): summed = lax.psum_scatter(piece, 'col', scatter_dimension=0, tiled=True)  93.6 us
    all_gather x1, waiting for transfers between devices, local(): lax.all_gather(normed.astype(jnp.bfloat16), 'col', axis=0, tiled=True)  51.8 us
    all_to_all x1, starting transfers between devices, local(): lax.all_to_all(spread, 'col', split_axis=0, concat_axis=0, tiled=True)  13 us
    ppermute x1, waiting for transfers between devices, local(): gate_far = lax.ppermute(w_gate[0], 'row', swap)  11.4 us
    all_to_all x1, waiting for transfers between devices, local(): lax.all_to_all(spread, 'col', split_axis=0, concat_axis=0, tiled=True)  10.6 us
    ppermute x1, waiting for transfers between devices, local(): lax.ppermute(mixed, 'section', [(i, (i + 1) % sections) for i in range(se...  9.98 us
    ppermute x1, starting transfers between devices, local(): up_far = lax.ppermute(w_up[0], 'row', swap)  7.59 us
    dot_general x1, matrix products, local(): both = jnp.dot(gathered, first, preferred_element_type=jnp.float32)  7.49 us
  transfers between devices with their start and end apart: 7, of which 5 were waited for; matrix products, arithmetic and copies ran while one was open for 4% of the time, Pallas kernels for 0%

profile of v1, /device:TPU:16, one launch (start us, length us, event | category | flops | bytes accessed | tf_op | source)
XLA Modules:
  0.0 239.5 jit_solution(8362973081753462403)
XLA Ops:
  6.5 0.0 all-gather.2.cloned.1.call-start
  6.5 0.8 convert_reduce_fusion
  7.3 1.2 fusion.13
  8.5 2.0 fusion.15
  10.5 0.0 all-gather.2.cloned.1.call-update
  10.5 7.6 %collective-permute-start.1 = (bf16[3584,128]{1,0:T(8,128)(2,1)}, bf16[3584,128]{1,0:T(8,128)(2,1)S(1)}, u32[]{:S(2)}, u32[]{:S(2)}) collective-permute-start(bf16[3584,128]{1,0:T(8,128)(2,1)} %bitcast.15), channel_id=1, source_target_pairs={{0,16},{16,0},{1,17},{17,1},{2,18},{18,2},{3,19},{19,3},{4,20},{20... | collective-permute-start | bytes 2752520 | tf_op jit(solution)/shard_map/ppermute | solution.py:28
  18.1 1.9 collective-permute-start
  20.0 0.7 select_reduce_fusion
  20.8 0.1 broadcast_in_dim.44
  20.8 0.6 broadcast_in_dim.45
  21.4 13.0 %all-to-all-start = ((f32[16,1,256]{2,1,0:T(1,128)}), f32[16,1,256]{2,1,0:T(1,128)S(1)}, u32[]{:S(2)}, u32[]{:S(2)}) async-start(f32[16,1,256]{2,1,0:T(1,128)} %broadcast_in_dim.45), calls=%async_computation | async-start | bytes 32768 | tf_op jit(solution)/shard_map/all_to_all | solution.py:19
  34.5 0.0 reduce-scatter.2.cloned.1.call-start
  34.5 2.2 collective-permute-start.2
  36.8 10.6 %all-to-all-done = f32[16,1,256]{2,1,0:T(1,128)S(1)} async-done(((f32[16,1,256]{2,1,0:T(1,128)}), f32[16,1,256]{2,1,0:T(1,128)S(1)}, u32[]{:S(2)}, u32[]{:S(2)}) %all-to-all-start) | async-done | bytes 16416 | tf_op jit(solution)/shard_map/all_to_all | solution.py:19
  47.4 0.1 reshape.29
  47.5 0.1 dynamic-slice_reduce_fusion.1
  47.6 0.1 broadcast_in_dim.48
  47.7 0.1 broadcast_in_dim.46
  47.7 0.0 collective-permute-done.1
  47.7 11.4 %collective-permute-done = bf16[3584,128]{1,0:T(8,128)(2,1)S(1)} collective-permute-done((bf16[3584,128]{1,0:T(8,128)(2,1)}, bf16[3584,128]{1,0:T(8,128)(2,1)S(1)}, u32[]{:S(2)}, u32[]{:S(2)}) %collective-permute-start) | collective-permute-done | bytes 917536 | tf_op jit(solution)/shard_map/ppermute | solution.py:27
  59.2 51.8 %all-gather.2.cloned.1.call-done = bf16[1024,3584]{1,0:T(8,128)(2,1)} async-done(((bf16[64,3584]{1,0:T(8,128)(2,1)}), bf16[1024,3584]{1,0:T(8,128)(2,1)}) %all-gather.2.cloned.1.call-update) | async-done | bytes 7340048 | tf_op jit(solution)/shard_map/all_gather | solution.py:25
  111.0 7.5 %fusion = f32[1024,512]{1,0:T(8,128)S(1)} fusion(bf16[1024,3584]{1,0:T(8,128)(2,1)} %all-gather.2.cloned.1.call-done, bf16[3584,128]{1,0:T(8,128)(2,1)S(1)} %collective-permute-done.1, bf16[3584,128]{1,0:T(8,128)(2,1)} %bitcast.16, bf16[3584,128]{1,0:T(8,128)(2,1)S(1)} %collective-permute-done, bf16[3584,128]{1,0:T(8,128)(2,1)} %bitcast.18), kind=kOutput, calls=%fused_computation.1 | convolution fusion | flops 3772776448 | bytes 13107200 | tf_op jit(solution)/shard_map/dot_general | solution.py:42
  118.5 0.0 collective-permute-done.2
  118.5 0.2 broadcast_in_dim.49
  118.7 0.2 broadcast_in_dim.47
  118.9 6.3 %convolution_convert_fusion = bf16[1024,3584]{1,0:T(8,128)(2,1)} fusion(bf16[128,3584]{1,0:T(8,128)(2,1)} %collective-permute-done.2, bf16[128,3584]{1,0:T(8,128)(2,1)S(1)} %bitcast.20, f32[1024,512]{1,0:T(8,128)S(1)} %fusion, f32[1024,128]{1,0:T(8,128)S(1)} %broadcast_in_dim.49, f32[1024,128]{1,0:T(8,128)S(1)} %broadcast_in_dim.47), kind=kOutput, calls=%fused_computation | convolution fusion | flops 1888485376 | bytes 12320768 | tf_op jit(solution)/shard_map/dot_general | solution.py:45
  125.2 0.0 reduce-scatter.2.cloned.1.call-update
  125.3 93.6 %reduce-scatter.2.cloned.1.call-done = bf16[64,3584]{1,0:T(8,128)(2,1)} async-done(((bf16[1024,3584]{1,0:T(8,128)(2,1)}), bf16[64,3584]{1,0:T(8,128)(2,1)}) %reduce-scatter.2.cloned.1.call-update) | async-done | bytes 458768 | tf_op jit(solution)/shard_map/reduce_scatter | solution.py:46
  218.9 1.1 fusion.19
  220.0 1.9 collective-permute-start.3
  221.9 10.0 %collective-permute-done.3 = bf16[1,64,3584]{2,1,0:T(8,128)(2,1)S(1)} collective-permute-done((bf16[1,64,3584]{2,1,0:T(8,128)(2,1)S(1)}, bf16[1,64,3584]{2,1,0:T(8,128)(2,1)S(1)}, u32[]{:S(2)}, u32[]{:S(2)}) %collective-permute-start.3) | collective-permute-done | bytes 458784 | tf_op jit(solution)/shard_map/ppermute | solution.py:49
  231.9 0.8 copy.11
  (6 shorter events, 0.1 us)
Async XLA Ops:
  6.5 104.5 %all-gather.2.cloned.1.call-start = ((), (), s32[]{:S(2)}) async-start(), calls=%async_computation.2 | async-start | bytes 7798784 | tf_op jit(solution)/shard_map/all_gather | solution.py:25
  10.5 37.2 %collective-permute-start.1 = (bf16[3584,128]{1,0:T(8,128)(2,1)}, bf16[3584,128]{1,0:T(8,128)(2,1)S(1)}, u32[]{:S(2)}, u32[]{:S(2)}) collective-permute-start(bf16[3584,128]{1,0:T(8,128)(2,1)} %bitcast.15), channel_id=1, source_target_pairs={{0,16},{16,0},{1,17},{17,1},{2,18},{18,2},{3,19},{19,3},{4,20},{20... | collective-permute-start | bytes 2752520 | tf_op jit(solution)/shard_map/ppermute | solution.py:28
  18.1 41.1 %collective-permute-start = (bf16[3584,128]{1,0:T(8,128)(2,1)}, bf16[3584,128]{1,0:T(8,128)(2,1)S(1)}, u32[]{:S(2)}, u32[]{:S(2)}) collective-permute-start(bf16[3584,128]{1,0:T(8,128)(2,1)} %bitcast.17), channel_id=1, source_target_pairs={{0,16},{16,0},{1,17},{17,1},{2,18},{18,2},{3,19},{19,3},{4,20},{20... | collective-permute-start | bytes 2752520 | tf_op jit(solution)/shard_map/ppermute | solution.py:27
  21.4 26.0 %all-to-all-start = ((f32[16,1,256]{2,1,0:T(1,128)}), f32[16,1,256]{2,1,0:T(1,128)S(1)}, u32[]{:S(2)}, u32[]{:S(2)}) async-start(f32[16,1,256]{2,1,0:T(1,128)} %broadcast_in_dim.45), calls=%async_computation | async-start | bytes 32768 | tf_op jit(solution)/shard_map/all_to_all | solution.py:19
  34.5 184.4 %reduce-scatter.2.cloned.1.call-start = ((), (), s32[]{:S(2)}) async-start(), calls=%async_computation.3 | async-start | bytes 7798784 | tf_op jit(solution)/shard_map/reduce_scatter | solution.py:46
  34.5 84.0 %collective-permute-start.2 = (bf16[128,3584]{1,0:T(8,128)(2,1)}, bf16[128,3584]{1,0:T(8,128)(2,1)}, u32[]{:S(2)}, u32[]{:S(2)}) collective-permute-start(bf16[128,3584]{1,0:T(8,128)(2,1)} %bitcast.19), channel_id=1, source_target_pairs={{0,16},{16,0},{1,17},{17,1},{2,18},{18,2},{3,19},{19,3},{4,20},{20... | collective-permute-start | bytes 2752520 | tf_op jit(solution)/shard_map/ppermute | solution.py:29
  47.7 71.2 %copy-start.1 = (bf16[1,128,3584]{2,1,0:T(8,128)(2,1)S(1)}, bf16[1,128,3584]{2,1,0:T(8,128)(2,1)}, u32[]{:S(2)}) copy-start(bf16[1,128,3584]{2,1,0:T(8,128)(2,1)} %param.12) | copy-start | bytes 2752516
  125.2 93.7 %copy-start = (bf16[1,64,3584]{2,1,0:T(8,128)(2,1)S(1)}, bf16[1,64,3584]{2,1,0:T(8,128)(2,1)}, u32[]{:S(2)}) copy-start(bf16[1,64,3584]{2,1,0:T(8,128)(2,1)} %param.8) | copy-start | bytes 1376260
  220.0 11.9 %collective-permute-start.3 = (bf16[1,64,3584]{2,1,0:T(8,128)(2,1)S(1)}, bf16[1,64,3584]{2,1,0:T(8,128)(2,1)S(1)}, u32[]{:S(2)}, u32[]{:S(2)}) collective-permute-start(bf16[1,64,3584]{2,1,0:T(8,128)(2,1)S(1)} %fusion.19), channel_id=1, source_target_pairs={{0,32},{32,64},{64,96},{96,128},{128,160},{160,192},{192,224},{224... | collective-permute-start | bytes 1376264 | tf_op jit(solution)/shard_map/ppermute | solution.py:49
Sparse Core Ops, SparseCore 0:
  10.6 100.3 all-gather.1
  125.4 93.4 reduce-scatter.1

commit v2 on v1

v2 whole, which is shorter than its diff:
```python
import jax
import jax.numpy as jnp
from jax import lax
from jax.experimental import pallas as pl
from jax.experimental.pallas import tpu as pltpu
from jax.sharding import Mesh
from jax.sharding import PartitionSpec as P

EXPERTS = 4
ROW_TILE = 256
COLUMN_TILE = 512


def norm_kernel(token_ref, gain_ref, out_ref):
    values = token_ref[...].astype(jnp.float32)
    mean_sq = jnp.mean(values * values, axis=-1, keepdims=True)
    scale = lax.rsqrt(mean_sq + 1e-06)
    out_ref[...] = (values * scale * gain_ref[...].astype(jnp.float32)).astype(out_ref.dtype)


def normalise(tokens, gain):
    return pl.pallas_call(
        norm_kernel,
        out_shape=jax.ShapeDtypeStruct(tokens.shape, tokens.dtype),
        in_specs=[pl.BlockSpec(memory_space=pltpu.VMEM)] * 2,
        out_specs=pl.BlockSpec(memory_space=pltpu.VMEM),
        name="normalise",
    )(tokens, gain)


def expert_kernel(row_ref, near_ref, far_ref, first_ref, second_ref, out_ref, w1, w2, sems):
    copies = (
        pltpu.make_async_copy(first_ref, w1, sems.at[0]),
        pltpu.make_async_copy(second_ref, w2, sems.at[1]),
    )

    @pl.when(pl.program_id(0) == 0)
    def _():
        for copy in copies:
            copy.start()
        copies[0].wait()

    both = jnp.dot(row_ref[...], w1[...], preferred_element_type=jnp.float32)
    half, units = both.shape[1] // 2, near_ref.shape[1]
    gate, up = both[:, :half], both[:, half:]
    hidden = gate / (1.0 + jnp.exp(-gate)) * up
    hidden = jnp.concatenate(
        [hidden[:, :units] * near_ref[...], hidden[:, units:] * far_ref[...]], axis=1
    ).astype(jnp.bfloat16)

    @pl.when(pl.program_id(0) == 0)
    def _():
        copies[1].wait()

    for at in range(0, out_ref.shape[1], COLUMN_TILE):
        span = slice(at, at + COLUMN_TILE)
        piece = jnp.dot(hidden, w2[:, span], preferred_element_type=jnp.float32)
        out_ref[:, span] = piece.astype(out_ref.dtype)


def expert_sums(gathered, near, far, first, second):
    count, width = gathered.shape
    tile = min(ROW_TILE, count)

    def tiled(columns):
        return pl.BlockSpec((tile, columns), lambda i: (i, 0))

    return pl.pallas_call(
        expert_kernel,
        grid=(count // tile,),
        out_shape=jax.ShapeDtypeStruct(gathered.shape, gathered.dtype),
        in_specs=[
            tiled(width),
            tiled(near.shape[1]),
            tiled(far.shape[1]),
            pl.BlockSpec(memory_space=pl.ANY),
            pl.BlockSpec(memory_space=pl.ANY),
        ],
        out_specs=tiled(width),
        scratch_shapes=[
            pltpu.VMEM(first.shape, first.dtype),
            pltpu.VMEM(second.shape, second.dtype),
            pltpu.SemaphoreType.DMA((2,)),
        ],
        compiler_params=pltpu.CompilerParams(vmem_limit_bytes=58 * 1024 * 1024),
        cost_estimate=pl.CostEstimate(
            flops=2 * count * (first.size + second.size),
            bytes_accessed=2 * gathered.size * 2,
            transcendentals=count * first.shape[1] // 2,
        ),
        name="expert_sums",
    )(gathered, near, far, first, second)


def onward(value):
    sections = lax.axis_size("section")
    return lax.ppermute(value, "section", [(i, (i + 1) % sections) for i in range(sections)])


def local(tokens, norm_gain, w_gate, w_up, w_down, expert_ids, slot_ids, route_weight):
    row, col = lax.axis_index("row"), lax.axis_index("col")
    rows, cols = lax.axis_size("row"), lax.axis_size("col")
    count = tokens.shape[1]
    swap = [(0, 1), (1, 0)]

    named = expert_ids[0][None] == jnp.arange(EXPERTS, dtype=jnp.int32)[:, None, None]
    dense = jnp.sum(jnp.where(named, route_weight[0][None], 0.0), axis=2)
    spread = jnp.broadcast_to(dense.reshape(1, -1), (cols, EXPERTS * count))
    spread = lax.all_to_all(spread, "col", split_axis=0, concat_axis=0, tiled=True)
    spread = spread.reshape(cols, EXPERTS, count)

    normed = normalise(tokens[0], norm_gain)
    gathered = lax.all_gather(normed, "col", axis=0, tiled=True)

    gate_far = lax.ppermute(w_gate[0], "row", swap)
    up_far = lax.ppermute(w_up[0], "row", swap)
    down_far = lax.ppermute(w_down[0], "row", swap)
    first = jnp.concatenate([w_gate[0], gate_far, w_up[0], up_far], axis=1)
    second = jnp.concatenate([w_down[0], down_far], axis=0)
    per_row = EXPERTS // rows
    mine = col // (cols // per_row)

    def weight_of(expert):
        picked = lax.dynamic_index_in_dim(spread, expert, 1, keepdims=False)
        return jnp.broadcast_to(picked.reshape(-1, 1), (cols * count, w_gate.shape[2]))

    near, far = weight_of(row * per_row + mine), weight_of((1 - row) * per_row + mine)
    first, second, near, far = lax.optimization_barrier((first, second, near, far))
    piece = expert_sums(gathered, near, far, first, second)
    summed = lax.psum_scatter(piece, "col", scatter_dimension=0, tiled=True)
    mixed = onward(tokens[0]).astype(jnp.float32) + onward(summed).astype(jnp.float32)
    return mixed.astype(jnp.bfloat16)[None]


def solution(mesh):
    sections, members = mesh.devices.shape
    fine = Mesh(mesh.devices.reshape(sections, 2, members // 2), ("section", "row", "col"))
    split = ("row", "col")
    placed = (
        P("section", split, None),
        P("section", None),
        P("section", None, split),
        P("section", None, split),
        P("section", split, None),
        P("section", split, None),
        P("section", split, None),
        P("section", split, None),
    )
    return jax.shard_map(
        local, mesh=fine, in_specs=placed, out_specs=P("section", split, None), check_vma=False
    )
```

time: 240 us -> 236 us (0.983)
  Pallas kernels: 0 us -> 14.9 us
  matrix products: 13.8 us -> 0 us
  waiting for transfers between devices: 177 us -> 167 us
    all_gather x1, waiting for transfers between devices: 51.8 us -> 30.9 us  [local(): gathered = lax.all_gather(normed, 'col', axis=0, tiled=True)]
    ppermute x1, waiting for transfers between devices: 0.01 us -> 16.5 us  [local(): up_far = lax.ppermute(w_up[0], 'row', swap)]
    pallas_call x0 -> x2, Pallas kernels: none -> 14.9 us  [the longest x1 12.7 us: expert_sums(): pl.pallas_call(expert_kernel, grid=(count // tile,), out_shape=jax.ShapeD...]
    dot_general x2 -> x0, matrix products: 13.8 us -> none  [the longest x1 7.49 us: local(): both = jnp.dot(gathered, first, preferred_element_type=jnp.float32)]
    concatenate x0 -> x2, other arithmetic: none -> 5.89 us  [the longest x1 3.06 us: local(): first = jnp.concatenate([w_gate[0], gate_far, w_up[0], up_far], axis=1)]
    ppermute x1, starting transfers between devices: 2.25 us -> 7.59 us  [local(): down_far = lax.ppermute(w_down[0], 'row', swap)]
    ppermute x1, waiting for transfers between devices: 11.4 us -> 6.32 us  [local(): gate_far = lax.ppermute(w_gate[0], 'row', swap)]
    all_to_all x1, starting transfers between devices: 13 us -> 9.85 us  [local(): lax.all_to_all(spread, 'col', split_axis=0, concat_axis=0, tiled=True)]
  transfers between devices with their start and end apart: 7 -> 8, of which waited for: 5 -> 6; matrix products, arithmetic and copies ran while one was open for 4% -> 4% of each run, Pallas kernels for 0% -> 0%
where the time goes in v2:
time: 236 us
  waiting for transfers between devices  167 us (71%)
  starting transfers between devices  28.7 us (12%)
  Pallas kernels  14.9 us (6%)
  between operations  13.5 us (6%)
  other arithmetic  7.51 us (3%)
  local copies, waits for them, and re-layouts  3.96 us (2%)
    reduce_scatter x1, waiting for transfers between devices, local(): summed = lax.psum_scatter(piece, 'col', scatter_dimension=0, tiled=True)  90.7 us
    all_gather x1, waiting for transfers between devices, local(): gathered = lax.all_gather(normed, 'col', axis=0, tiled=True)  30.9 us
    ppermute x1, waiting for transfers between devices, local(): up_far = lax.ppermute(w_up[0], 'row', swap)  16.5 us
    all_to_all x1, waiting for transfers between devices, local(): lax.all_to_all(spread, 'col', split_axis=0, concat_axis=0, tiled=True)  12.9 us
    pallas_call x1, Pallas kernels, expert_sums(): pl.pallas_call(expert_kernel, grid=(count // tile,), out_shape=jax.ShapeD...  12.7 us
    ppermute x2, waiting for transfers between devices, onward(): lax.ppermute(value, 'section', [(i, (i + 1) % sections) for i in range(se...  10.2 us
    all_to_all x1, starting transfers between devices, local(): lax.all_to_all(spread, 'col', split_axis=0, concat_axis=0, tiled=True)  9.85 us
    ppermute x1, starting transfers between devices, local(): down_far = lax.ppermute(w_down[0], 'row', swap)  7.59 us
  transfers between devices with their start and end apart: 8, of which 6 were waited for; matrix products, arithmetic and copies ran while one was open for 4% of the time, Pallas kernels for 0%

profile of v2, /device:TPU:16, one launch (start us, length us, event | category | flops | bytes accessed | tf_op | source)
XLA Modules:
  0.0 236.0 jit_solution(15763293128284324620)
XLA Ops:
  6.5 2.2 normalise.1
  8.7 0.0 all-gather.2.cloned.1.call-update
  8.7 7.6 %collective-permute-start.3 = (bf16[128,3584]{1,0:T(8,128)(2,1)}, bf16[128,3584]{1,0:T(8,128)(2,1)}, u32[]{:S(2)}, u32[]{:S(2)}) collective-permute-start(bf16[128,3584]{1,0:T(8,128)(2,1)} %bitcast.8), channel_id=1, source_target_pairs={{0,16},{16,0},{1,17},{17,1},{2,18},{18,2},{3,19},{19,3},{4,20},{20... | collective-permute-start | bytes 2752520 | tf_op jit(solution)/shard_map/ppermute | solution.py:117
  16.3 1.9 collective-permute-start.1
  18.3 5.4 %collective-permute-start.2 = (bf16[3584,128]{1,0:T(8,128)(2,1)}, bf16[3584,128]{1,0:T(8,128)(2,1)}, u32[]{:S(2)}, u32[]{:S(2)}) collective-permute-start(bf16[3584,128]{1,0:T(8,128)(2,1)} %bitcast.10), channel_id=1, source_target_pairs={{0,16},{16,0},{1,17},{17,1},{2,18},{18,2},{3,19},{19,3},{4,20},{20... | collective-permute-start | bytes 2752520 | tf_op jit(solution)/shard_map/ppermute | solution.py:116
  23.7 0.7 select_reduce_fusion
  24.4 0.1 broadcast_in_dim.42
  24.5 0.6 broadcast_in_dim.43
  25.1 9.8 %all-to-all-start = ((f32[16,1,256]{2,1,0:T(1,128)}), f32[16,1,256]{2,1,0:T(1,128)S(1)}, u32[]{:S(2)}, u32[]{:S(2)}) async-start(f32[16,1,256]{2,1,0:T(1,128)} %broadcast_in_dim.43), calls=%async_computation | async-start | bytes 32768 | tf_op jit(solution)/shard_map/all_to_all | solution.py:109
  35.0 0.0 reduce-scatter.2.cloned.1.call-start
  35.1 12.9 %all-to-all-done = f32[16,1,256]{2,1,0:T(1,128)S(1)} async-done(((f32[16,1,256]{2,1,0:T(1,128)}), f32[16,1,256]{2,1,0:T(1,128)S(1)}, u32[]{:S(2)}, u32[]{:S(2)}) %all-to-all-start) | async-done | bytes 16416 | tf_op jit(solution)/shard_map/all_to_all | solution.py:109
  48.0 0.1 reshape.19
  48.0 0.1 dynamic-slice_reduce_fusion
  48.1 0.1 broadcast_in_dim.44
  48.2 0.1 broadcast_in_dim.46
  48.3 2.8 %pad_maximum_fusion.1.second_ref = bf16[256,3584]{1,0:T(8,128)(2,1)} fusion(bf16[128,3584]{1,0:T(8,128)(2,1)} %collective-permute-done.3, bf16[128,3584]{1,0:T(8,128)(2,1)} %bitcast.9), kind=kLoop, calls=%fused_computation.1 | loop fusion | flops 3670016 | bytes 3670016 | tf_op jit(solution)/shard_map/concatenate | solution.py:119
  51.1 6.3 %collective-permute-done.1 = bf16[3584,128]{1,0:T(8,128)(2,1)S(1)} collective-permute-done((bf16[3584,128]{1,0:T(8,128)(2,1)}, bf16[3584,128]{1,0:T(8,128)(2,1)S(1)}, u32[]{:S(2)}, u32[]{:S(2)}) %collective-permute-start.1) | collective-permute-done | bytes 917536 | tf_op jit(solution)/shard_map/ppermute | solution.py:115
  57.4 16.5 %collective-permute-done.2 = bf16[3584,128]{1,0:T(8,128)(2,1)} collective-permute-done((bf16[3584,128]{1,0:T(8,128)(2,1)}, bf16[3584,128]{1,0:T(8,128)(2,1)}, u32[]{:S(2)}, u32[]{:S(2)}) %collective-permute-start.2) | collective-permute-done | bytes 917536 | tf_op jit(solution)/shard_map/ppermute | solution.py:116
  73.9 3.1 %pad_maximum_fusion.first_ref = bf16[3584,512]{1,0:T(8,128)(2,1)} fusion(bf16[3584,128]{1,0:T(8,128)(2,1)} %collective-permute-done.2, bf16[3584,128]{1,0:T(8,128)(2,1)S(1)} %bitcast.11, bf16[3584,128]{1,0:T(8,128)(2,1)S(1)} %collective-permute-done.1, bf16[3584,128]{1,0:T(8,128)(2,1)S(1)} %bitcast.13), kind=kLoop, calls=%fused_computation | loop fusion | flops 14680064 | bytes 7340032 | tf_op jit(solution)/shard_map/concatenate | solution.py:118
  76.9 1.0 broadcast_in_dim.45.near_ref
  77.9 1.0 broadcast_in_dim.47.far_ref
  78.9 30.9 %all-gather.2.cloned.1.call-done.row_ref = bf16[1024,3584]{1,0:T(8,128)(2,1)} async-done(((bf16[64,3584]{1,0:T(8,128)(2,1)}), bf16[1024,3584]{1,0:T(8,128)(2,1)}) %all-gather.2.cloned.1.call-update) | async-done | bytes 7340048 | tf_op jit(solution)/shard_map/all_gather | solution.py:113
  109.8 12.7 %expert_sums.1 = bf16[1024,3584]{1,0:T(8,128)(2,1)} custom-call(bf16[1024,3584]{1,0:T(8,128)(2,1)} %all-gather.2.cloned.1.call-done.row_ref, f32[1024,128]{1,0:T(8,128)} %broadcast_in_dim.45.near_ref, f32[1024,128]{1,0:T(8,128)} %broadcast_in_dim.47.far_ref, bf16[3584,512]{1,0:T(8,128)(2,1)} %pad_maximum_fusion.first_ref, ...), custom_call_target="tpu_custom_call" | custom-call | flops 5637144576 | bytes 14680064 | tf_op jit(solution)/shard_map/expert_sums/pallas_call | solution.py:68
  122.5 0.0 copy-start.2
  122.5 0.0 reduce-scatter.2.cloned.1.call-update
  122.6 1.0 copy-done.2
  123.5 1.9 collective-permute-start
  125.5 90.7 %reduce-scatter.2.cloned.1.call-done = bf16[64,3584]{1,0:T(8,128)(2,1)} async-done(((bf16[1024,3584]{1,0:T(8,128)(2,1)}), bf16[64,3584]{1,0:T(8,128)(2,1)}) %reduce-scatter.2.cloned.1.call-update) | async-done | bytes 458768 | tf_op jit(solution)/shard_map/reduce_scatter | solution.py:130
  216.2 1.9 collective-permute-start.4
  218.1 0.0 collective-permute-done
  218.1 10.2 %collective-permute-done.4 = bf16[64,3584]{1,0:T(8,128)(2,1)S(1)} collective-permute-done((bf16[64,3584]{1,0:T(8,128)(2,1)}, bf16[64,3584]{1,0:T(8,128)(2,1)S(1)}, u32[]{:S(2)}, u32[]{:S(2)}) %collective-permute-start.4) | collective-permute-done | bytes 458784 | tf_op jit(solution)/shard_map/ppermute | solution.py:97
  228.3 0.9 fusion
  (7 shorter events, 0.1 us)
Async XLA Ops:
  6.5 67.3 %copy-start.1 = (bf16[1,3584,128]{2,1,0:T(8,128)(2,1)S(1)}, bf16[1,3584,128]{2,1,0:T(8,128)(2,1)}, u32[]{:S(2)}) copy-start(bf16[1,3584,128]{2,1,0:T(8,128)(2,1)} %param.10) | copy-start | bytes 2752516
  6.5 67.3 %copy-start = (bf16[1,3584,128]{2,1,0:T(8,128)(2,1)S(1)}, bf16[1,3584,128]{2,1,0:T(8,128)(2,1)}, u32[]{:S(2)}) copy-start(bf16[1,3584,128]{2,1,0:T(8,128)(2,1)} %param.11) | copy-start | bytes 2752516
  6.5 103.2 %all-gather.2.cloned.1.call-start = ((), (), s32[]{:S(2)}) async-start(), calls=%async_computation.2 | async-start | bytes 7798784 | tf_op jit(solution)/shard_map/all_gather | solution.py:113
  8.7 39.5 %collective-permute-start.3 = (bf16[128,3584]{1,0:T(8,128)(2,1)}, bf16[128,3584]{1,0:T(8,128)(2,1)}, u32[]{:S(2)}, u32[]{:S(2)}) collective-permute-start(bf16[128,3584]{1,0:T(8,128)(2,1)} %bitcast.8), channel_id=1, source_target_pairs={{0,16},{16,0},{1,17},{17,1},{2,18},{18,2},{3,19},{19,3},{4,20},{20... | collective-permute-start | bytes 2752520 | tf_op jit(solution)/shard_map/ppermute | solution.py:117
  16.3 41.1 %collective-permute-start.1 = (bf16[3584,128]{1,0:T(8,128)(2,1)}, bf16[3584,128]{1,0:T(8,128)(2,1)S(1)}, u32[]{:S(2)}, u32[]{:S(2)}) collective-permute-start(bf16[3584,128]{1,0:T(8,128)(2,1)} %bitcast.12), channel_id=1, source_target_pairs={{0,16},{16,0},{1,17},{17,1},{2,18},{18,2},{3,19},{19,3},{4,20},{20... | collective-permute-start | bytes 2752520 | tf_op jit(solution)/shard_map/ppermute | solution.py:115
  18.3 55.6 %collective-permute-start.2 = (bf16[3584,128]{1,0:T(8,128)(2,1)}, bf16[3584,128]{1,0:T(8,128)(2,1)}, u32[]{:S(2)}, u32[]{:S(2)}) collective-permute-start(bf16[3584,128]{1,0:T(8,128)(2,1)} %bitcast.10), channel_id=1, source_target_pairs={{0,16},{16,0},{1,17},{17,1},{2,18},{18,2},{3,19},{19,3},{4,20},{20... | collective-permute-start | bytes 2752520 | tf_op jit(solution)/shard_map/ppermute | solution.py:116
  25.1 22.8 %all-to-all-start = ((f32[16,1,256]{2,1,0:T(1,128)}), f32[16,1,256]{2,1,0:T(1,128)S(1)}, u32[]{:S(2)}, u32[]{:S(2)}) async-start(f32[16,1,256]{2,1,0:T(1,128)} %broadcast_in_dim.43), calls=%async_computation | async-start | bytes 32768 | tf_op jit(solution)/shard_map/all_to_all | solution.py:109
  35.0 181.2 %reduce-scatter.2.cloned.1.call-start = ((), (), s32[]{:S(2)}) async-start(), calls=%async_computation.3 | async-start | bytes 7798784 | tf_op jit(solution)/shard_map/reduce_scatter | solution.py:130
  122.5 1.0 copy-start.2
  123.5 94.6 %collective-permute-start = (bf16[64,3584]{1,0:T(8,128)(2,1)S(1)}, bf16[64,3584]{1,0:T(8,128)(2,1)S(1)}, u32[]{:S(2)}, u32[]{:S(2)}) collective-permute-start(bf16[64,3584]{1,0:T(8,128)(2,1)S(1)} %bitcast.15), channel_id=1, source_target_pairs={{0,32},{32,64},{64,96},{96,128},{128,160},{160,192},{192,224},{224... | collective-permute-start | bytes 1376264 | tf_op jit(solution)/shard_map/ppermute | solution.py:97
  216.2 12.1 %collective-permute-start.4 = (bf16[64,3584]{1,0:T(8,128)(2,1)}, bf16[64,3584]{1,0:T(8,128)(2,1)S(1)}, u32[]{:S(2)}, u32[]{:S(2)}) collective-permute-start(bf16[64,3584]{1,0:T(8,128)(2,1)} %reduce-scatter.2.cloned.1.call-done), channel_id=1, source_target_pairs={{0,32},{32,64},{64,96},{96,128},{128,160},{160,192},{192,224},{224... | collective-permute-start | bytes 1376264 | tf_op jit(solution)/shard_map/ppermute | solution.py:97
Sparse Core Ops, SparseCore 0:
  9.4 100.3 all-gather.1
  122.7 93.4 reduce-scatter.1

commit v3 on v1

--- a/solution.py
+++ b/solution.py
@@ -1,16 +1,40 @@
 import jax
 import jax.numpy as jnp
 from jax import lax
+from jax.experimental import pallas as pl
+from jax.experimental.pallas import tpu as pltpu
 from jax.sharding import Mesh
 from jax.sharding import PartitionSpec as P
 
 EXPERTS = 4
 
 
+def norm_kernel(token_ref, gain_ref, out_ref):
+    values = token_ref[...].astype(jnp.float32)
+    mean_sq = jnp.mean(values * values, axis=-1, keepdims=True)
+    scale = lax.rsqrt(mean_sq + 1e-06)
+    out_ref[...] = (values * scale * gain_ref[...].astype(jnp.float32)).astype(out_ref.dtype)
+
+
+def normalise(tokens, gain):
+    return pl.pallas_call(
+        norm_kernel,
+        out_shape=jax.ShapeDtypeStruct(tokens.shape, tokens.dtype),
+        in_specs=[pl.BlockSpec(memory_space=pltpu.VMEM)] * 2,
+        out_specs=pl.BlockSpec(memory_space=pltpu.VMEM),
+        name="normalise",
+    )(tokens, gain)
+
+
+def onward(value):
+    sections = lax.axis_size("section")
+    return lax.ppermute(value, "section", [(i, (i + 1) % sections) for i in range(sections)])
+
+
 def local(tokens, norm_gain, w_gate, w_up, w_down, expert_ids, slot_ids, route_weight):
     row, col = lax.axis_index("row"), lax.axis_index("col")
     rows, cols = lax.axis_size("row"), lax.axis_size("col")
-    count, width = tokens.shape[1:]
+    count = tokens.shape[1]
     swap = [(0, 1), (1, 0)]
 
     named = expert_ids[0][None] == jnp.arange(EXPERTS, dtype=jnp.int32)[:, None, None]
@@ -19,16 +43,15 @@
     spread = lax.all_to_all(spread, "col", split_axis=0, concat_axis=0, tiled=True)
     spread = spread.reshape(cols, EXPERTS, count)
 
-    values = tokens[0].astype(jnp.float32)
-    mean_sq = jnp.mean(values * values, axis=-1, keepdims=True)
-    normed = values * lax.rsqrt(mean_sq + 1e-06) * norm_gain[0].astype(jnp.float32)
-    gathered = lax.all_gather(normed.astype(jnp.bfloat16), "col", axis=0, tiled=True)
+    normed = normalise(tokens[0], norm_gain)
+    gathered = lax.all_gather(normed, "col", axis=0, tiled=True)
 
     gate_far = lax.ppermute(w_gate[0], "row", swap)
     up_far = lax.ppermute(w_up[0], "row", swap)
     down_far = lax.ppermute(w_down[0], "row", swap)
     first = jnp.concatenate([w_gate[0], gate_far, w_up[0], up_far], axis=1)
     second = jnp.concatenate([w_down[0], down_far], axis=0)
+    first, second = lax.optimization_barrier((first, second))
     per_row = EXPERTS // rows
     mine = col // (cols // per_row)
 
@@ -44,9 +67,8 @@
     hidden = (jax.nn.silu(both[:, :half]) * both[:, half:] * weights).astype(jnp.bfloat16)
     piece = jnp.dot(hidden, second, preferred_element_type=jnp.float32).astype(jnp.bfloat16)
     summed = lax.psum_scatter(piece, "col", scatter_dimension=0, tiled=True)
-    mixed = (values + summed.astype(jnp.float32)).astype(jnp.bfloat16)[None]
-    sections = lax.axis_size("section")
-    return lax.ppermute(mixed, "section", [(i, (i + 1) % sections) for i in range(sections)])
+    mixed = onward(tokens[0]).astype(jnp.float32) + onward(summed).astype(jnp.float32)
+    return mixed.astype(jnp.bfloat16)[None]
 
 
 def solution(mesh):

time: 240 us -> 236 us (0.983)
  waiting for transfers between devices: 177 us -> 170 us
    all_gather x1, waiting for transfers between devices: 51.8 us -> 32.7 us  [local(): gathered = lax.all_gather(normed, 'col', axis=0, tiled=True)]
    ppermute x1, waiting for transfers between devices: 0.01 us -> 7.6 us  [local(): up_far = lax.ppermute(w_up[0], 'row', swap)]
    ppermute x1, starting transfers between devices: 7.59 us -> 1.92 us  [local(): up_far = lax.ppermute(w_up[0], 'row', swap)]
    ppermute x1, starting transfers between devices: 2.25 us -> 7.59 us  [local(): down_far = lax.ppermute(w_down[0], 'row', swap)]
    concatenate x0 -> x2, other arithmetic: none -> 4.97 us  [the longest x1 3.28 us: local(): first = jnp.concatenate([w_gate[0], gate_far, w_up[0], up_far], axis=1)]
    ppermute x1, waiting for transfers between devices: 11.4 us -> 16.4 us  [local(): gate_far = lax.ppermute(w_gate[0], 'row', swap)]
    ppermute x1, starting transfers between devices: 1.92 us -> 5.43 us  [local(): gate_far = lax.ppermute(w_gate[0], 'row', swap)]
    all_to_all x1, starting transfers between devices: 13 us -> 9.85 us  [local(): lax.all_to_all(spread, 'col', split_axis=0, concat_axis=0, tiled=True)]
  transfers between devices with their start and end apart: 7 -> 8, of which waited for: 5 -> 6; matrix products, arithmetic and copies ran while one was open for 4% -> 3% of each run, Pallas kernels for 0% -> 0%
where the time goes in v3:
time: 236 us
  waiting for transfers between devices  170 us (72%)
  starting transfers between devices  28.7 us (12%)
  between operations  13.5 us (6%)
  matrix products  12.4 us (5%)
  other arithmetic  6.59 us (3%)
  local copies, waits for them, and re-layouts  2.36 us (1%)
    reduce_scatter x1, waiting for transfers between devices, local(): summed = lax.psum_scatter(piece, 'col', scatter_dimension=0, tiled=True)  90.7 us
    all_gather x1, waiting for transfers between devices, local(): gathered = lax.all_gather(normed, 'col', axis=0, tiled=True)  32.7 us
    ppermute x1, waiting for transfers between devices, local(): gate_far = lax.ppermute(w_gate[0], 'row', swap)  16.4 us
    all_to_all x1, waiting for transfers between devices, local(): lax.all_to_all(spread, 'col', split_axis=0, concat_axis=0, tiled=True)  12.8 us
    ppermute x2, waiting for transfers between devices, onward(): lax.ppermute(value, 'section', [(i, (i + 1) % sections) for i in range(se...  10.2 us
    all_to_all x1, starting transfers between devices, local(): lax.all_to_all(spread, 'col', split_axis=0, concat_axis=0, tiled=True)  9.85 us
    ppermute x1, waiting for transfers between devices, local(): up_far = lax.ppermute(w_up[0], 'row', swap)  7.6 us
    ppermute x1, starting transfers between devices, local(): down_far = lax.ppermute(w_down[0], 'row', swap)  7.59 us
  transfers between devices with their start and end apart: 8, of which 6 were waited for; matrix products, arithmetic and copies ran while one was open for 3% of the time, Pallas kernels for 0%

profile of v3, /device:TPU:16, one launch (start us, length us, event | category | flops | bytes accessed | tf_op | source)
XLA Modules:
  0.0 236.1 jit_solution(616422859006041521)
XLA Ops:
  6.5 2.1 normalise.1
  8.7 0.0 all-gather.2.cloned.1.call-update
  8.7 7.6 %collective-permute-start.3 = (bf16[128,3584]{1,0:T(8,128)(2,1)}, bf16[128,3584]{1,0:T(8,128)(2,1)}, u32[]{:S(2)}, u32[]{:S(2)}) collective-permute-start(bf16[128,3584]{1,0:T(8,128)(2,1)} %bitcast.11), channel_id=1, source_target_pairs={{0,16},{16,0},{1,17},{17,1},{2,18},{18,2},{3,19},{19,3},{4,20},{20... | collective-permute-start | bytes 2752520 | tf_op jit(solution)/shard_map/ppermute | solution.py:51
  16.3 1.9 collective-permute-start.2
  18.2 5.4 %collective-permute-start.1 = (bf16[3584,128]{1,0:T(8,128)(2,1)}, bf16[3584,128]{1,0:T(8,128)(2,1)}, u32[]{:S(2)}, u32[]{:S(2)}) collective-permute-start(bf16[3584,128]{1,0:T(8,128)(2,1)} %bitcast.15), channel_id=1, source_target_pairs={{0,16},{16,0},{1,17},{17,1},{2,18},{18,2},{3,19},{19,3},{4,20},{20... | collective-permute-start | bytes 2752520 | tf_op jit(solution)/shard_map/ppermute | solution.py:49
  23.7 0.7 select_reduce_fusion
  24.4 0.1 broadcast_in_dim.42
  24.4 0.6 broadcast_in_dim.43
  25.1 9.8 %all-to-all-start = ((f32[16,1,256]{2,1,0:T(1,128)}), f32[16,1,256]{2,1,0:T(1,128)S(1)}, u32[]{:S(2)}, u32[]{:S(2)}) async-start(f32[16,1,256]{2,1,0:T(1,128)} %broadcast_in_dim.43), calls=%async_computation | async-start | bytes 32768 | tf_op jit(solution)/shard_map/all_to_all | solution.py:43
  34.9 0.0 reduce-scatter.2.cloned.1.call-start
  35.0 12.8 %all-to-all-done = f32[16,1,256]{2,1,0:T(1,128)S(1)} async-done(((f32[16,1,256]{2,1,0:T(1,128)}), f32[16,1,256]{2,1,0:T(1,128)S(1)}, u32[]{:S(2)}, u32[]{:S(2)}) %all-to-all-start) | async-done | bytes 16416 | tf_op jit(solution)/shard_map/all_to_all | solution.py:43
  47.9 0.1 reshape.19
  47.9 0.1 dynamic-slice_reduce_fusion.1
  48.0 0.1 broadcast_in_dim.46
  48.1 0.1 broadcast_in_dim.44
  48.2 0.0 collective-permute-done.3
  48.2 1.7 pad_maximum_fusion.1
  49.9 7.6 %collective-permute-done.2 = bf16[3584,128]{1,0:T(8,128)(2,1)} collective-permute-done((bf16[3584,128]{1,0:T(8,128)(2,1)}, bf16[3584,128]{1,0:T(8,128)(2,1)}, u32[]{:S(2)}, u32[]{:S(2)}) %collective-permute-start.2) | collective-permute-done | bytes 917536 | tf_op jit(solution)/shard_map/ppermute | solution.py:50
  57.4 16.4 %collective-permute-done.1 = bf16[3584,128]{1,0:T(8,128)(2,1)} collective-permute-done((bf16[3584,128]{1,0:T(8,128)(2,1)}, bf16[3584,128]{1,0:T(8,128)(2,1)}, u32[]{:S(2)}, u32[]{:S(2)}) %collective-permute-start.1) | collective-permute-done | bytes 917536 | tf_op jit(solution)/shard_map/ppermute | solution.py:49
  73.8 3.3 %pad_maximum_fusion = bf16[3584,512]{1,0:T(8,128)(2,1)} fusion(bf16[3584,128]{1,0:T(8,128)(2,1)} %collective-permute-done.2, bf16[3584,128]{1,0:T(8,128)(2,1)S(1)} %bitcast.14, bf16[3584,128]{1,0:T(8,128)(2,1)} %collective-permute-done.1, bf16[3584,128]{1,0:T(8,128)(2,1)S(1)} %bitcast.16), kind=kLoop, calls=%fused_computation.1 | loop fusion | flops 14680064 | bytes 7340032 | tf_op jit(solution)/shard_map/concatenate | solution.py:52
  77.1 32.7 %all-gather.2.cloned.1.call-done = bf16[1024,3584]{1,0:T(8,128)(2,1)} async-done(((bf16[64,3584]{1,0:T(8,128)(2,1)}), bf16[1024,3584]{1,0:T(8,128)(2,1)}) %all-gather.2.cloned.1.call-update) | async-done | bytes 7340048 | tf_op jit(solution)/shard_map/all_gather | solution.py:47
  109.8 7.3 %fusion.7 = f32[1024,512]{1,0:T(8,128)S(1)} fusion(bf16[1024,3584]{1,0:T(8,128)(2,1)} %all-gather.2.cloned.1.call-done, bf16[3584,512]{1,0:T(8,128)(2,1)} %pad_maximum_fusion), kind=kOutput, calls=%fused_computation.15 | convolution fusion | flops 3758096384 | bytes 13107200 | tf_op jit(solution)/shard_map/dot_general | solution.py:65
  117.1 0.2 broadcast_in_dim.47
  117.3 0.2 broadcast_in_dim.45
  117.5 5.1 %convolution_convert_fusion = bf16[1024,3584]{1,0:T(8,128)(2,1)} fusion(bf16[256,3584]{1,0:T(8,128)(2,1)S(1)} %pad_maximum_fusion.1, f32[1024,512]{1,0:T(8,128)S(1)} %fusion.7, f32[1024,128]{1,0:T(8,128)S(1)} %broadcast_in_dim.47, f32[1024,128]{1,0:T(8,128)S(1)} %broadcast_in_dim.45), kind=kOutput, calls=%fused_computation | convolution fusion | flops 1884815360 | bytes 12320768 | tf_op jit(solution)/shard_map/dot_general | solution.py:68
  122.6 0.0 reduce-scatter.2.cloned.1.call-update
  122.6 1.0 copy-done.2
  123.6 1.9 collective-permute-start
  125.5 90.7 %reduce-scatter.2.cloned.1.call-done = bf16[64,3584]{1,0:T(8,128)(2,1)} async-done(((bf16[1024,3584]{1,0:T(8,128)(2,1)}), bf16[64,3584]{1,0:T(8,128)(2,1)}) %reduce-scatter.2.cloned.1.call-update) | async-done | bytes 458768 | tf_op jit(solution)/shard_map/reduce_scatter | solution.py:69
  216.3 1.9 collective-permute-start.4
  218.2 10.2 %collective-permute-done.4 = bf16[64,3584]{1,0:T(8,128)(2,1)S(1)} collective-permute-done((bf16[64,3584]{1,0:T(8,128)(2,1)}, bf16[64,3584]{1,0:T(8,128)(2,1)S(1)}, u32[]{:S(2)}, u32[]{:S(2)}) %collective-permute-start.4) | collective-permute-done | bytes 458784 | tf_op jit(solution)/shard_map/ppermute | solution.py:31
  228.4 0.9 fusion.4
  (8 shorter events, 0.1 us)
Async XLA Ops:
  6.5 67.3 %copy-start = (bf16[1,3584,128]{2,1,0:T(8,128)(2,1)S(1)}, bf16[1,3584,128]{2,1,0:T(8,128)(2,1)}, u32[]{:S(2)}) copy-start(bf16[1,3584,128]{2,1,0:T(8,128)(2,1)} %param.11) | copy-start | bytes 2752516
  6.5 103.2 %all-gather.2.cloned.1.call-start = ((), (), s32[]{:S(2)}) async-start(), calls=%async_computation.2 | async-start | bytes 7798784 | tf_op jit(solution)/shard_map/all_gather | solution.py:47
  8.7 39.5 %collective-permute-start.3 = (bf16[128,3584]{1,0:T(8,128)(2,1)}, bf16[128,3584]{1,0:T(8,128)(2,1)}, u32[]{:S(2)}, u32[]{:S(2)}) collective-permute-start(bf16[128,3584]{1,0:T(8,128)(2,1)} %bitcast.11), channel_id=1, source_target_pairs={{0,16},{16,0},{1,17},{17,1},{2,18},{18,2},{3,19},{19,3},{4,20},{20... | collective-permute-start | bytes 2752520 | tf_op jit(solution)/shard_map/ppermute | solution.py:51
  16.3 41.2 %collective-permute-start.2 = (bf16[3584,128]{1,0:T(8,128)(2,1)}, bf16[3584,128]{1,0:T(8,128)(2,1)}, u32[]{:S(2)}, u32[]{:S(2)}) collective-permute-start(bf16[3584,128]{1,0:T(8,128)(2,1)} %bitcast.13), channel_id=1, source_target_pairs={{0,16},{16,0},{1,17},{17,1},{2,18},{18,2},{3,19},{19,3},{4,20},{20... | collective-permute-start | bytes 2752520 | tf_op jit(solution)/shard_map/ppermute | solution.py:50
  18.2 55.6 %collective-permute-start.1 = (bf16[3584,128]{1,0:T(8,128)(2,1)}, bf16[3584,128]{1,0:T(8,128)(2,1)}, u32[]{:S(2)}, u32[]{:S(2)}) collective-permute-start(bf16[3584,128]{1,0:T(8,128)(2,1)} %bitcast.15), channel_id=1, source_target_pairs={{0,16},{16,0},{1,17},{17,1},{2,18},{18,2},{3,19},{19,3},{4,20},{20... | collective-permute-start | bytes 2752520 | tf_op jit(solution)/shard_map/ppermute | solution.py:49
  25.1 22.8 %all-to-all-start = ((f32[16,1,256]{2,1,0:T(1,128)}), f32[16,1,256]{2,1,0:T(1,128)S(1)}, u32[]{:S(2)}, u32[]{:S(2)}) async-start(f32[16,1,256]{2,1,0:T(1,128)} %broadcast_in_dim.43), calls=%async_computation | async-start | bytes 32768 | tf_op jit(solution)/shard_map/all_to_all | solution.py:43
  34.9 181.3 %reduce-scatter.2.cloned.1.call-start = ((), (), s32[]{:S(2)}) async-start(), calls=%async_computation.3 | async-start | bytes 7798784 | tf_op jit(solution)/shard_map/reduce_scatter | solution.py:69
  48.2 25.7 %copy-start.1 = (bf16[1,3584,128]{2,1,0:T(8,128)(2,1)S(1)}, bf16[1,3584,128]{2,1,0:T(8,128)(2,1)}, u32[]{:S(2)}) copy-start(bf16[1,3584,128]{2,1,0:T(8,128)(2,1)} %param.10) | copy-start | bytes 2752516
  122.6 1.0 copy-start.2
  123.6 94.6 %collective-permute-start = (bf16[64,3584]{1,0:T(8,128)(2,1)S(1)}, bf16[64,3584]{1,0:T(8,128)(2,1)S(1)}, u32[]{:S(2)}, u32[]{:S(2)}) collective-permute-start(bf16[64,3584]{1,0:T(8,128)(2,1)S(1)} %bitcast.18), channel_id=1, source_target_pairs={{0,32},{32,64},{64,96},{96,128},{128,160},{160,192},{192,224},{224... | collective-permute-start | bytes 1376264 | tf_op jit(solution)/shard_map/ppermute | solution.py:31
  216.3 12.1 %collective-permute-start.4 = (bf16[64,3584]{1,0:T(8,128)(2,1)}, bf16[64,3584]{1,0:T(8,128)(2,1)S(1)}, u32[]{:S(2)}, u32[]{:S(2)}) collective-permute-start(bf16[64,3584]{1,0:T(8,128)(2,1)} %reduce-scatter.2.cloned.1.call-done), channel_id=1, source_target_pairs={{0,32},{32,64},{64,96},{96,128},{128,160},{160,192},{192,224},{224... | collective-permute-start | bytes 1376264 | tf_op jit(solution)/shard_map/ppermute | solution.py:31
Sparse Core Ops, SparseCore 0:
  9.4 100.3 all-gather.1
  122.8 93.4 reduce-scatter.1
